TPU v7x, 32 devices: a whole 2x2x4 slice. The times are simulated.
32 devices in a mesh: groups: 2 (over x), seq: 16 (over z, y, core).
Axes of the slice: x: 2, y: 2, z: 4, core: 2. Of those that a mesh axis runs over, the one named last changes fastest.
Arguments:
- queries: bfloat16 [4096, 1024], P(('groups', 'seq')), parts along dimension 0, may hold values from -6 to 6
- key_rows: bfloat16 [4096, 1024], P(('groups', 'seq')), parts along dimension 0, may hold values from -6 to 6
- value_rows: bfloat16 [4096, 1024], P(('groups', 'seq')), parts along dimension 0, may hold values from -6 to 6
- strength: float32 [4096, 8], P(('groups', 'seq')), parts along dimension 0, may hold values from 0 to 1, as said below
- conv_weight: bfloat16 [3, 4, 1024], replicated, may hold values from -3 to 3
- out_gain: float32 [128], replicated, may hold values from 0.5 to 1.5
Outputs:
- mixed: bfloat16 [4096, 1024], P(('groups', 'seq')), parts along dimension 0
There are 2 independent parts, one for each index of `groups`. A program takes and returns all parts, laid end to end along the dimension named above; an argument that names none is the same for every part. Nothing has to cross between parts.
Inputs may be any that keep to these rules, and one draw needn't show every extreme that they name: A write strength of each token and head, positive and at most one.
All inputs are finite; a program needn't handle non-finite values.
Results may differ from a plain program's by a relative error of at most 0.001.
Values may be sent and summed in bfloat16 or wider, within the bound.
No kernel may reach another device: no remote copies, remote signals or barrier semaphores. Data moves between devices by JAX's collectives and lax.ppermute only.
A program may use at most 192 MiB of HBM per device.

v0:
```python
import jax
import jax.numpy as jnp
from jax import lax
from jax.sharding import PartitionSpec as P

SPAN = 64


def from_behind(value, axis, steps):
    count = lax.axis_size(axis)
    first, last = (max(0, -steps), min(count, count - steps))
    return lax.ppermute(value, axis, [(source, source + steps) for source in range(first, last)])


def carried_in(part, axis, combine, identity):
    place = lax.axis_index(axis)
    gathered = jax.tree.map(lambda a: lax.all_gather(a, axis), part)
    state = jax.tree.map(lambda a, e: jnp.zeros_like(a) + jnp.asarray(e, a.dtype), part, identity)

    def one(hop, state):
        return combine(
            state, jax.tree.map(lambda a: lax.dynamic_index_in_dim(a, hop, 0, False), gathered)
        )

    return lax.fori_loop(0, place, one, state)


def multiply(form, left, right):
    return jnp.einsum(form, left, right, precision=lax.Precision.HIGHEST)


def unit_rows(values):
    return values / jnp.sqrt(jnp.sum(values * values, axis=-1, keepdims=True) + 1e-06)


def joint_step(stacked, pieces):
    key_block, erase_rows, write_rows = pieces
    depth = write_rows.shape[-1]
    moved = multiply("hid,hde->hie", erase_rows, stacked)
    update = jnp.concatenate([-moved[..., :depth], write_rows - moved[..., depth:]], axis=-1)
    return (stacked + multiply("hid,hie->hde", key_block, update), None)


def output_step(memory, pieces):
    query_block, key_block, erase_rows, write_rows, scores = pieces
    delta = write_rows - multiply("hid,hde->hie", erase_rows, memory)
    output = multiply("hid,hde->hie", query_block, memory) + multiply("hij,hje->hie", scores, delta)
    return (memory + multiply("hid,hie->hde", key_block, delta), output)


def combine(earlier, later):
    transit = multiply("hij,hjk->hik", later[0], earlier[0])
    memory = multiply("hij,hjk->hik", later[0], earlier[1]) + later[1]
    return (transit, memory)


def shards(queries, key_rows, value_rows, strength, conv_weight, out_gain):
    width = conv_weight.shape[1] - 1
    tails = jnp.stack([queries[-width:], key_rows[-width:], value_rows[-width:]])
    earlier_rows = from_behind(tails, "seq", 1)
    tokens = queries.shape[0]
    heads = strength.shape[1]
    depth = queries.shape[1] // heads
    blocks = tokens // SPAN
    mixed_heads = []
    for index, source in enumerate((queries, key_rows, value_rows)):
        extended = jnp.concatenate([earlier_rows[index], source], axis=0).astype(jnp.float32)
        kernel = conv_weight[index].astype(jnp.float32)
        summed = extended[0:tokens] * kernel[0]
        for offset in range(1, width + 1):
            summed = summed + extended[offset : offset + tokens] * kernel[offset]
        mixed_heads.append(
            jax.nn.silu(summed).reshape(blocks, SPAN, heads, depth).transpose(0, 2, 1, 3)
        )
    query_blocks = unit_rows(mixed_heads[0])
    key_blocks = unit_rows(mixed_heads[1])
    value_blocks = mixed_heads[2]
    decay_rates = strength.reshape(blocks, SPAN, heads).transpose(0, 2, 1)
    identity_span = jnp.eye(SPAN, dtype=jnp.float32)
    strict_lower = jnp.tril(jnp.ones((SPAN, SPAN), jnp.float32), -1)
    with_diagonal = jnp.tril(jnp.ones((SPAN, SPAN), jnp.float32), 0)
    gram = multiply("nhid,nhjd->nhij", key_blocks, key_blocks)
    nilpotent = gram * decay_rates[..., :, None] * strict_lower
    inverse = identity_span - nilpotent
    power = nilpotent
    exponent = 1
    while 2 * exponent < SPAN:
        power = multiply("nhij,nhjk->nhik", power, power)
        exponent = 2 * exponent
        inverse = multiply("nhij,nhjk->nhik", inverse, identity_span + power)
    weighted = inverse * decay_rates[..., None, :]
    erase_rows = multiply("nhij,nhjd->nhid", weighted, key_blocks)
    write_rows = multiply("nhij,nhjd->nhid", weighted, value_blocks)
    scores = multiply("nhid,nhjd->nhij", query_blocks, key_blocks) * with_diagonal
    zero_memory = jnp.zeros((heads, depth, depth), jnp.float32)
    identity_memory = jnp.broadcast_to(jnp.eye(depth, dtype=jnp.float32), (heads, depth, depth))
    final_memory, local_outputs = lax.scan(
        output_step, zero_memory, (query_blocks, key_blocks, erase_rows, write_rows, scores)
    )
    transit_only, unused = lax.scan(
        joint_step,
        jnp.concatenate([identity_memory, zero_memory], axis=-1),
        (key_blocks, erase_rows, jnp.zeros_like(write_rows)),
    )
    transit = transit_only[..., :depth]
    prefix = carried_in((transit, final_memory), "seq", combine, (identity_memory, zero_memory))
    unused_memory, corrections = lax.scan(
        output_step,
        prefix[1],
        (query_blocks, key_blocks, erase_rows, jnp.zeros_like(write_rows), scores),
    )
    outputs = local_outputs + corrections
    normed = (
        outputs * lax.rsqrt(jnp.mean(outputs * outputs, axis=-1, keepdims=True) + 1e-05) * out_gain
    )
    return normed.astype(jnp.bfloat16).transpose(0, 2, 1, 3).reshape(tokens, heads * depth)


def solution(mesh):
    placed = (
        P(("groups", "seq"), None),
        P(("groups", "seq"), None),
        P(("groups", "seq"), None),
        P(("groups", "seq"), None),
        P(),
        P(),
    )
    return jax.shard_map(
        shards, mesh=mesh, in_specs=placed, out_specs=P(("groups", "seq"), None), check_vma=False
    )
```

profile of v0, /device:TPU:29, one launch (start us, length us, event | category | flops | bytes accessed | tf_op | source)
XLA Modules:
  0.0 221.3 jit_solution(16992618943700472050)
XLA Ops:
  8.0 1.3 collective-permute-start
  22.4 4.1 %while.47 = (s32[]{:T(128)}, f32[8,128,256]{2,1,0:T(8,128)S(1)}, f32[2,8,64,128]{3,2,1,0:T(8,128)S(1)}, f32[2,8,64,128]{3,2,1,0:T(8,128)S(1)}, s32[]{:T(128)}) while((s32[]{:T(128)}, f32[8,128,256]{2,1,0:T(8,128)S(1)}, f32[2,8,64,128]{3,2,1,0:T(8,128)S(1)}, f32[2,8,64,128]{3,2,1,0:T(8,128)S(1)}, s32[]{:T(128)}) %tuple.95), condition=%wide.region_5.6_spmd, body=%wide.region_4.5_spmd.sunk | while | flops 403177472 | bytes 5767245 | solution.py:100
  23.2 1.3 convolution_add_fusion.11
  25.3 1.3 convolution_add_fusion.11
  30.3 2.6 %fusion.68 = f32[2,8,64,128]{3,2,1,0:T(8,128)} fusion(f32[2,8,64,64]{3,2,1,0:T(8,128)} %copy-done.1, f32[2,64,8,128]{3,2,1,0:T(8,128)S(1)} %bitcast.207), kind=kOutput, calls=%fused_computation.96 | convolution fusion | flops 100663296 | bytes 1310720 | tf_op jit(solution)/shard_map/nhij,nhjd->nhid/dot_general | solution.py:29
  34.7 8.7 %while.50 = (s32[]{:T(128)}, f32[8,128,128]{2,1,0:T(8,128)S(1)}, f32[2,8,64,128]{3,2,1,0:T(8,128)}, f32[2,8,64,128]{3,2,1,0:T(8,128)S(1)}, f32[2,8,64,128]{3,2,1...) while((s32[]{:T(128)}, f32[8,128,128]{2,1,0:T(8,128)S(1)}, ...), condition=%wide.region_3.4_spmd.clone, body=%wide.region_2.3_spmd.clone.sunk | while | flops 352976896 | bytes 4983424 | solution.py:97
  35.3 1.5 convolution_subtract_fusion.5
  36.9 1.1 convolution_add_fusion.14
  38.0 1.1 fusion.179
  39.7 1.6 convolution_subtract_fusion.5
  41.2 1.1 convolution_add_fusion.14
  42.3 1.1 fusion.179
  44.2 58.5 %all-gather.5.cloned.1.call-done = f32[128,128,128]{2,1,0:T(8,128)} async-done(((f32[8,128,128]{2,1,0:T(8,128)}), f32[128,128,128]{2,1,0:T(8,128)}) %all-gather.5.cloned.1.call-update) | async-done | bytes 8388624 | tf_op jit(solution)/shard_map/all_gather | solution.py:17
  102.7 75.1 %all-gather.7.cloned.1.call-done = f32[128,128,128]{2,1,0:T(8,128)} async-done(((f32[8,128,128]{2,1,0:T(8,128)}), f32[128,128,128]{2,1,0:T(8,128)}) %all-gather.7.cloned.1.call-update) | async-done | bytes 8388624 | tf_op jit(solution)/shard_map/all_gather | solution.py:17
  177.9 28.8 %while.48 = (s32[]{:T(128)}, f32[8,128,128]{2,1,0:T(8,128)S(1)}, s32[]{:T(128)}, f32[16,8,128,128]{3,2,1,0:T(8,128)}, f32[16,8,128,128]{3,2,1,0:T(8,128)}, /*index=5*/s32[]{:T(128)}, s32[]{:T(128)}, s32[]{:T(128)}) while((s32[]{:T(128)}, f32[8,128,128]{2,1,0:T(8,128)S(1)}, s32[]{:T(128)}, f32[16,8,128,128]{3,2,1,0:T(8,128)}, ...), condition=%wide.region_7.8_spmd, body=%wide.region_6.7_spmd.sunk | while | flops 201457664 | bytes 3146879 | solution.py:25
  177.9 1.8 convolution_add_fusion.12
  179.8 1.8 convolution_add_fusion.12
  181.8 1.8 convolution_add_fusion.12
  183.7 1.8 convolution_add_fusion.12
  185.6 1.8 convolution_add_fusion.12
  187.5 1.8 convolution_add_fusion.12
  189.5 1.8 convolution_add_fusion.12
  191.4 1.8 convolution_add_fusion.12
  193.3 1.8 convolution_add_fusion.12
  195.2 1.8 convolution_add_fusion.12
  197.1 1.8 convolution_add_fusion.12
  199.1 1.8 convolution_add_fusion.12
  201.0 1.8 convolution_add_fusion.12
  202.9 1.8 convolution_add_fusion.12
  204.8 1.8 convolution_add_fusion.12
  206.8 5.3 %while.49 = (s32[]{:T(128)}, f32[8,128,128]{2,1,0:T(8,128)S(1)}, f32[2,8,64,128]{3,2,1,0:T(8,128)S(1)}, f32[2,8,64,128]{3,2,1,0:T(8,128)S(1)}, f32[2,8,64,128]{3...) while((s32[]{:T(128)}, f32[8,128,128]{2,1,0:T(8,128)S(1)}, ...), condition=%wide.region_9.10_spmd, body=%wide.region_8.9_spmd.sunk | while | flops 352583680 | bytes 4719721 | solution.py:97
  212.1 1.3 multiply_reduce_fusion
  (97 shorter events, 30.3 us)
Async XLA Ops:
  6.5 96.2 %all-gather.5.cloned.1.call-start = ((), (), s32[]{:S(2)}) async-start(), calls=%async_computation | async-start | bytes 8912896 | tf_op jit(solution)/shard_map/all_gather | solution.py:17
  8.0 3.3 %collective-permute-start = (bf16[3,3,1024]{2,1,0:T(4,128)(2,1)S(1)}, bf16[3,3,1024]{2,1,0:T(4,128)(2,1)S(1)}, u32[]{:S(2)}, u32[]{:S(2)}) collective-permute-start(bf16[3,3,1024]{2,1,0:T(4,128)(2,1)S(1)} %pad_maximum_fusion), channel_id=1, source_target_pairs={{0,1},{1,2},{2,3},{3,4},{4,5},{5,6},{6,7},{7,8},{8,9},{9,10},{10,1... | collective-permute-start | bytes 55304 | tf_op jit(solution)/shard_map/ppermute | solution.py:12
  20.9 0.8 copy-start.1
  22.4 5.3 %copy-start.2 = (bf16[128,1024]{1,0:T(8,128)(2,1)S(1)}, bf16[128,1024]{1,0:T(8,128)(2,1)}, u32[]{:S(2)}) copy-start(bf16[128,1024]{1,0:T(8,128)(2,1)} %param.16) | copy-start | bytes 786436
  27.4 150.4 %all-gather.7.cloned.1.call-start = ((), (), s32[]{:S(2)}) async-start(), calls=%async_computation.1 | async-start | bytes 8912896 | tf_op jit(solution)/shard_map/all_gather | solution.py:17
  43.4 0.8 copy-start
  206.7 6.6 %copy-start.3 = (f32[128]{0:T(128)S(1)}, f32[128]{0:T(128)}, u32[]{:S(2)}) copy-start(f32[128]{0:T(128)} %param.19) | copy-start | bytes 1540
Sparse Core Ops, SparseCore 0:
  27.5 75.1 all-gather.4
  104.9 72.8 all-gather.6
where the time goes:
time: 222 us; the launch traced here: 221 us
  waiting for transfers between devices  134 us (60%)
  matrix products  57.3 us (26%)
  between operations  13.8 us (6%)
  local copies, waits for them, and re-layouts  7.8 us (4%)
  other arithmetic  6.37 us (3%)
    all_gather x2, waiting for transfers between devices, carried_in(): gathered = jax.tree.map(lambda a: lax.all_gather(a, axis), part)  134 us
    dot_general x49, matrix products, multiply(): return jnp.einsum(form, left, right, precision=lax.Precision.HIGHEST)  57.3 us
  transfers between devices with their start and end apart: 3, of which 3 were waited for; matrix products, arithmetic and copies ran while one was open for 8% of the time, Pallas kernels for 0%

commit v1 on v0

v1 whole, which is shorter than its diff:
```python
import functools

import jax
import jax.numpy as jnp
from jax import lax
from jax.experimental import pallas as pl
from jax.experimental.pallas import tpu as pltpu
from jax.sharding import PartitionSpec as P

EXTRA = 16
F32 = jnp.float32
BF16 = jnp.bfloat16


def split(x):
    high = x.astype(BF16)
    return high, (x - high.astype(F32)).astype(BF16)


def left(parts):
    return jnp.concatenate(parts, axis=1)


def right(parts):
    both = jnp.concatenate(parts, axis=1)
    return jnp.concatenate([both, both], axis=0)


def product(lhs, rhs):
    both = lax.dot_general(lhs, rhs, (((1,), (0,)), ((), ())), preferred_element_type=F32)
    half = both.shape[1] // 2
    return both[:, :half] + both[:, half:]


def product_t(a, b):
    dims = (((1,), (1,)), ((), ()))
    lhs = jnp.concatenate(a, axis=1)
    rhs_high = jnp.concatenate([b[0], b[0]], axis=1)
    rhs_low = jnp.concatenate([b[1], b[1]], axis=1)
    both = lax.dot_general(
        lhs, jnp.concatenate([rhs_high, rhs_low], axis=0), dims, preferred_element_type=F32
    )
    half = both.shape[1] // 2
    return both[:, :half] + both[:, half:]


def rows_kernel(width, raw_ref, taps_ref, local_ref, carry_ref, final_ref, ext_ref):
    chunks, _, depth = raw_ref.shape
    span = (raw_ref.shape[1] - EXTRA) // 3
    row = lax.broadcasted_iota(jnp.int32, (span, span), 0)
    col = lax.broadcasted_iota(jnp.int32, (span, span), 1)
    eye = (row == col).astype(F32)

    def activated(c, index, extra):
        base = index * 1
        ext_ref[base, 8 - width : 8, :] = extra[index * width : (index + 1) * width]
        ext_ref[base, 8 : 8 + span, :] = raw_ref[c, index * span : (index + 1) * span, :].astype(F32)
        total = None
        for tap in range(width + 1):
            term = ext_ref[base, 8 - width + tap : 8 - width + tap + span, :] * taps_ref[
                index * (width + 1) + tap : index * (width + 1) + tap + 1, :
            ]
            total = term if total is None else total + term
        return total / (1.0 + jnp.exp(-total))

    def unit(x):
        return x * lax.rsqrt(jnp.sum(x * x, axis=-1, keepdims=True) + 1e-06)

    state = None
    stage = []
    for c in range(chunks):
        extra = raw_ref[c, 3 * span :, :].astype(F32)
        query = unit(activated(c, 0, extra))
        key = unit(activated(c, 1, extra))
        value = activated(c, 2, extra)
        at = 3 * width
        rate_row = extra[at : at + 1] + extra[at + 1 : at + 2] + extra[at + 2 : at + 3]
        rate = jnp.sum(eye * rate_row, axis=1, keepdims=True)
        key_parts = split(key)
        scores = jnp.where(row >= col, product_t(split(query), key_parts), 0.0)
        lower = jnp.where(row > col, rate * product_t(key_parts, key_parts), 0.0)
        stage.append((query, key, value, rate, scores, lower))
    inverses = []
    for c in range(chunks):
        lower = stage[c][5]
        inverses.append(eye - jnp.where((row ^ col) == 1, lower, 0.0))
    size = 2
    while size < span:
        for c in range(chunks):
            pick = ((row ^ col) < 2 * size) & ((row & size) != (col & size))
            block = jnp.where(pick, stage[c][5], 0.0)
            parts = split(inverses[c])
            inner = product(left(split(block)), right(parts))
            inverses[c] = inverses[c] - product(left(parts), right(split(inner)))
        size *= 2
    for c in range(chunks):
        query, key, value, rate, scores, lower = stage[c]
        both = jnp.concatenate([rate * key, rate * value], axis=1)
        solved = product(left(split(inverses[c])), right(split(both)))
        solved = right(split(solved))
        moved = product(left(split(key.T)), solved)
        shown = product(left(split(scores)), solved)
        seen = query - shown[:, :depth]
        if c == 0:
            local_ref[c] = shown[:, depth:]
            carry_ref[c] = seen
            state = jnp.concatenate([eye - moved[:, :depth], moved[:, depth:]], axis=1)
        else:
            state_parts = right(split(state))
            out = product(left(split(seen)), state_parts)
            carry_ref[c] = out[:, :depth]
            local_ref[c] = shown[:, depth:] + out[:, depth:]
            through = product(left(split(eye - moved[:, :depth])), state_parts)
            state = jnp.concatenate([through[:, :depth], through[:, depth:] + moved[:, depth:]], axis=1)
    final_ref[0] = state[:, :depth]
    final_ref[1] = state[:, depth:]


def finish_kernel(local_ref, carry_ref, memory_ref, gain_ref, out_ref):
    chunks = local_ref.shape[0]
    memory = right(split(memory_ref[...]))
    gain = gain_ref[...]
    for c in range(chunks):
        output = local_ref[c] + product(left(split(carry_ref[c])), memory)
        scale = lax.rsqrt(jnp.mean(output * output, axis=-1, keepdims=True) + 1e-05)
        out_ref[c] = (output * scale * gain).astype(BF16)


def compose(later, earlier):
    join = functools.partial(jnp.einsum, "ij,jk->ik", precision=lax.Precision.HIGHEST)
    return jnp.stack([join(later[0], earlier[0]), join(later[0], earlier[1]) + later[1]])


def shards(queries, key_rows, value_rows, strength, conv_weight, out_gain):
    taps = conv_weight.shape[1]
    width = taps - 1
    span, heads = strength.shape
    depth = queries.shape[1] // heads
    count = lax.axis_size("seq")
    place = lax.axis_index("seq")
    blocks = count // heads
    assert blocks * heads == count
    groups = [[b * heads + h for h in range(heads)] for b in range(blocks)]
    block, head = place // heads, place % heads

    def by_head(x):
        return x.reshape(-1, heads, depth).transpose(1, 0, 2)

    tails = jnp.concatenate([queries[-width:], key_rows[-width:], value_rows[-width:]])
    tails = lax.ppermute(tails, "seq", [(i, i + 1) for i in range(count - 1)])
    high = lax.reduce_precision(strength, 8, 7)
    rest = strength - high
    middle = lax.reduce_precision(rest, 8, 7)
    rates = jnp.stack([high.T, middle.T, (rest - middle).T], axis=1).astype(BF16)
    pad = jnp.zeros((heads, EXTRA - 3 * width - 3, depth), BF16)
    payload = jnp.concatenate(
        [by_head(queries), by_head(key_rows), by_head(value_rows), by_head(tails), rates, pad], axis=1
    )
    raw = lax.all_to_all(payload, "seq", 0, 0, axis_index_groups=groups, tiled=True)
    kernel_taps = lax.dynamic_slice_in_dim(
        conv_weight.reshape(3 * taps, heads * depth), head * depth, depth, 1
    ).astype(F32)

    whole = pl.BlockSpec(memory_space=pltpu.VMEM)
    local, carry, final = pl.pallas_call(
        functools.partial(rows_kernel, width),
        out_shape=(
            jax.ShapeDtypeStruct((heads, span, depth), F32),
            jax.ShapeDtypeStruct((heads, span, depth), F32),
            jax.ShapeDtypeStruct((2, depth, depth), F32),
        ),
        in_specs=[whole] * 2,
        out_specs=[whole] * 3,
        scratch_shapes=[pltpu.VMEM((3, span + 8, depth), F32)],
        name="rows",
    )(raw, kernel_taps)

    ring = [(i, (i + heads) % count) for i in range(count)]
    if blocks == 2:
        memory = lax.ppermute(final[1], "seq", ring)
        memory = jnp.where(block > 0, memory, 0.0)
    else:
        start = jnp.stack([jnp.eye(depth, dtype=F32), jnp.zeros((depth, depth), F32)])
        arrived = lax.ppermute(final, "seq", ring)
        prefix = jnp.where(block > 0, arrived, start)
        step = 1
        while step < blocks - 1:
            shift = [(i, (i + step * heads) % count) for i in range(count)]
            arrived = lax.ppermute(prefix, "seq", shift)
            prefix = jnp.where(block >= step, compose(prefix, arrived), prefix)
            step *= 2
        memory = prefix[1]

    mixed = pl.pallas_call(
        finish_kernel,
        out_shape=jax.ShapeDtypeStruct((heads, span, depth), BF16),
        in_specs=[whole] * 4,
        out_specs=whole,
        name="finish",
    )(local, carry, memory, out_gain.reshape(1, depth))
    mixed = lax.all_to_all(mixed, "seq", 0, 0, axis_index_groups=groups, tiled=True)
    return mixed.transpose(1, 0, 2).reshape(span, heads * depth)


def solution(mesh):
    placed = (
        P(("groups", "seq"), None),
        P(("groups", "seq"), None),
        P(("groups", "seq"), None),
        P(("groups", "seq"), None),
        P(),
        P(),
    )
    return jax.shard_map(
        shards, mesh=mesh, in_specs=placed, out_specs=P(("groups", "seq"), None), check_vma=False
    )
```

time: 222 us -> 60.6 us (0.27)
  the two profiles are of different devices: /device:TPU:29 before, /device:TPU:0 now
where the time goes in v1:
time: 60.6 us; the launch traced here: 59.8 us
  waiting for transfers between devices  13.5 us (22%)
  local copies, waits for them, and re-layouts  12.8 us (21%)
  Pallas kernels  11.7 us (19%)
  starting transfers between devices  10.7 us (18%)
  blocking collectives  9.55 us (16%)
  other arithmetic  1.27 us (2%)
    all_to_all x1, waiting for transfers between devices, shards(): lax.all_to_all(payload, 'seq', 0, 0, axis_index_groups=groups, tiled=True)  10.7 us
    all_to_all x1, blocking collectives, shards(): lax.all_to_all(mixed, 'seq', 0, 0, axis_index_groups=groups, tiled=True)  9.55 us
    pallas_call x1, Pallas kernels, shards(): pl.pallas_call(functools.partial(rows_kernel, width), out_shape=(jax.Shap...  9.43 us
    all_to_all x1, starting transfers between devices, shards(): lax.all_to_all(payload, 'seq', 0, 0, axis_index_groups=groups, tiled=True)  6.03 us
    concatenate x1, local copies, waits for them, and re-layouts, shards(): jnp.concatenate([by_head(queries), by_head(key_rows), by_head(value_rows)...  4.28 us
    unnamed x14, local copies, waits for them, and re-layouts  3.9 us
    ppermute x1, waiting for transfers between devices, shards(): memory = lax.ppermute(final[1], 'seq', ring)  2.89 us
    ppermute x1, starting transfers between devices, shards(): tails = lax.ppermute(tails, 'seq', [(i, i + 1) for i in range(count - 1)])  2.4 us
  transfers between devices with their start and end apart: 3, of which 2 were waited for; matrix products, arithmetic and copies ran while one was open for 4% of the time, Pallas kernels for 0%

profile of v1, /device:TPU:0, one launch (start us, length us, event | category | flops | bytes accessed | tf_op | source)
XLA Modules:
  0.0 59.8 jit_solution(861623618887975428)
XLA Ops:
  0.0 0.7 %slice.12 = bf16[3,1024]{1,0:T(4,128)(2,1)S(1)} slice(bf16[128,1024]{1,0:T(8,128)(2,1)} %param.6), slice={[125:128], [0:1024]} | slice | bytes 12288 | tf_op jit(solution)/shard_map/slice | solution.py:149
  0.7 0.7 %slice.13 = bf16[3,1024]{1,0:T(4,128)(2,1)S(1)} slice(bf16[128,1024]{1,0:T(8,128)(2,1)} %param.7), slice={[125:128], [0:1024]} | slice | bytes 12288 | tf_op jit(solution)/shard_map/slice | solution.py:149
  1.4 0.7 %slice.14 = bf16[3,1024]{1,0:T(4,128)(2,1)S(1)} slice(bf16[128,1024]{1,0:T(8,128)(2,1)} %param.8), slice={[125:128], [0:1024]} | slice | bytes 12288 | tf_op jit(solution)/shard_map/slice | solution.py:149
  2.2 0.0 copy-start.4
  2.2 2.4 %collective-permute-start = (bf16[9,1024]{1,0:T(8,128)(2,1)S(1)}, bf16[9,1024]{1,0:T(8,128)(2,1)S(1)}, u32[]{:S(2)}, u32[]{:S(2)}) collective-permute-start(bf16[9,1024]{1,0:T(8,128)(2,1)S(1)} %pad_maximum_fusion), channel_id=1, source_target_pairs={{0,1},{1,2},{2,3},{3,4},{4,5},{5,6},{6,7},{7,8},{8,9},{9,10},{10,1... | collective-permute-start | bytes 55304 | tf_op jit(solution)/shard_map/ppermute | solution.py:150
  4.6 0.0 copy-done.4
  4.6 0.0 copy-start.1
  4.7 1.2 %copy.31 = bf16[128,1024]{0,1:T(8,128)(2,1)S(1)} copy(bf16[128,1024]{1,0:T(8,128)(2,1)} %param.6) | data formatting | bytes 524288 | tf_op args[0]
  5.8 0.0 copy-done.1
  5.8 0.0 copy-start.2
  5.8 0.2 copy.33
  6.0 0.8 %copy-done.2 = bf16[128,1024]{1,0:T(8,128)(2,1)S(1)} copy-done((bf16[128,1024]{1,0:T(8,128)(2,1)S(1)}, bf16[128,1024]{1,0:T(8,128)(2,1)}, u32[]{:S(2)}) %copy-start.2) | copy-done | bytes 262168
  6.8 0.2 copy.35
  7.0 0.2 copy.32
  7.2 0.2 copy.34
  7.4 0.2 copy.36
  7.6 0.0 collective-permute-done
  7.6 4.3 %concatenate.8 = bf16[8,400,128]{2,1,0:T(8,128)(2,1)} concatenate(bf16[8,128,128]{2,1,0:T(8,128)(2,1)S(1)} %bitcast.29, bf16[8,128,128]{2,1,0:T(8,128)(2,1)S(1)} %bitcast.30, bf16[8,128,128]{2,1,0:T(8,128)(2,1)S(1)} %bitcast.31, bf16[8,9,128]{2,1,0:T(8,128)(2,1)S(1)} %bitcast.37, bf16[8,1,128]{2,1,0:T(2,128)(2,1)S(1)} %copy.38, bf16[8,1,128]{2,1,0:T(2,128)(2,1)S(1)} %copy.39, ...), dimensions={1} | concatenate | bytes 1638400 | tf_op jit(solution)/shard_map/concatenate | solution.py:156
  11.9 6.0 %all-to-all-start = ((bf16[8,400,128]{2,1,0:T(8,128)(2,1)}), bf16[8,400,128]{2,1,0:T(8,128)(2,1)S(1)}, u32[]{:S(2)}, u32[]{:S(2)}) async-start(bf16[8,400,128]{2,1,0:T(8,128)(2,1)} %concatenate.8), calls=%async_computation | async-start | bytes 1638400 | tf_op jit(solution)/shard_map/all_to_all | solution.py:159
  18.0 0.7 %copy-done.3 = bf16[3,4,1024]{2,1,0:T(4,128)(2,1)S(1)} copy-done((bf16[3,4,1024]{2,1,0:T(4,128)(2,1)S(1)}, bf16[3,4,1024]{2,1,0:T(4,128)(2,1)}, u32[]{:S(2)}) %copy-start.3) | copy-done | bytes 24600
  18.7 0.6 %dynamic-slice_convert_fusion.taps_ref = f32[12,128]{1,0:T(8,128)} fusion(bf16[12,1024]{1,0:T(8,128)(2,1)S(1)} %reshape.25, s32[]{:T(128)S(6)} %select_n.23), kind=kLoop, calls=%fused_computation.9 | loop fusion | flops 1536 | bytes 9220 | tf_op jit(solution)/shard_map/convert_element_type | solution.py:162
  19.3 10.7 %all-to-all-done.raw_ref = bf16[8,400,128]{2,1,0:T(8,128)(2,1)S(1)} async-done(((bf16[8,400,128]{2,1,0:T(8,128)(2,1)}), bf16[8,400,128]{2,1,0:T(8,128)(2,1)S(1)}, u32[]{:S(2)}, u32[]{:S(2)}) %all-to-all-start) | async-done | bytes 819232 | tf_op jit(solution)/shard_map/all_to_all | solution.py:159
  30.0 0.9 %copy-done = bf16[8,400,128]{2,1,0:T(8,128)(2,1)} copy-done((bf16[8,400,128]{2,1,0:T(8,128)(2,1)}, bf16[8,400,128]{2,1,0:T(8,128)(2,1)S(1)}, u32[]{:S(2)}) %copy-start) | copy-done | bytes 819224
  30.9 9.4 %rows.1 = (f32[8,128,128]{2,1,0:T(8,128)}, f32[8,128,128]{2,1,0:T(8,128)}, f32[2,128,128]{2,1,0:T(8,128)}) custom-call(bf16[8,400,128]{2,1,0:T(8,128)(2,1)} %copy-done, f32[12,128]{1,0:T(8,128)} %dynamic-slice_convert_fusion.taps_ref), custom_call_target="tpu_custom_call" | custom-call | tf_op jit(solution)/shard_map/rows/pallas_call | solution.py:165
  40.3 0.8 %slice_bitcast_fusion = f32[128,128]{1,0:T(8,128)S(1)} fusion(f32[2,128,128]{2,1,0:T(8,128)} %get-tuple-element.10), kind=kLoop, calls=%fused_computation | loop fusion | bytes 131072 | tf_op jit(solution)/shard_map/squeeze | solution.py:180
  41.1 2.3 %collective-permute-start.1 = (f32[128,128]{1,0:T(8,128)S(1)}, f32[128,128]{1,0:T(8,128)S(1)}, u32[]{:S(2)}, u32[]{:S(2)}) collective-permute-start(f32[128,128]{1,0:T(8,128)S(1)} %slice_bitcast_fusion), channel_id=1, source_target_pairs={{0,8},{1,9},{2,10},{3,11},{4,12},{5,13},{6,14},{7,15},{8,0},{9,1},... | collective-permute-start | bytes 196616 | tf_op jit(solution)/shard_map/ppermute | solution.py:180
  43.4 2.9 %collective-permute-done.1 = f32[128,128]{1,0:T(8,128)S(1)} collective-permute-done((f32[128,128]{1,0:T(8,128)S(1)}, f32[128,128]{1,0:T(8,128)S(1)}, u32[]{:S(2)}, u32[]{:S(2)}) %collective-permute-start.1) | collective-permute-done | bytes 65568 | tf_op jit(solution)/shard_map/ppermute | solution.py:180
  46.3 0.6 %broadcast_select_fusion.memory_ref = f32[128,128]{1,0:T(8,128)} fusion(f32[128,128]{1,0:T(8,128)S(1)} %collective-permute-done.1, pred[]{:T(512)S(6)} %gt.3), kind=kLoop, calls=%fused_computation.3 | loop fusion | flops 16384 | bytes 131073 | tf_op jit(solution)/shard_map/jit(_where)/select_n | solution.py:181
  46.9 2.3 %finish.1 = bf16[8,128,128]{2,1,0:T(8,128)(2,1)} custom-call(f32[8,128,128]{2,1,0:T(8,128)} %get-tuple-element.8.local_ref, f32[8,128,128]{2,1,0:T(8,128)} %get-tuple-element.9.carry_ref, f32[128,128]{1,0:T(8,128)} %broadcast_select_fusion.memory_ref, f32[1,128]{1,0:T(1,128)} %bitcast.40), custom_call_target="tpu_custom_call" | custom-call | tf_op jit(solution)/shard_map/finish/pallas_call | solution.py:194
  49.2 9.5 %all_to_all.10 = bf16[8,128,128]{2,1,0:T(8,128)(2,1)S(1)} all-to-all(bf16[8,128,128]{2,1,0:T(8,128)(2,1)} %finish.1), channel_id=1, replica_groups={{0,1,2,3,4,5,6,7},{8,9,10,11,12,13,14,15},{16,17,18,19,20,21,22,23},{24..., dimensions={0} | all-to-all | bytes 524288 | tf_op jit(solution)/shard_map/all_to_all | solution.py:201
  58.8 0.2 copy.41
  59.0 0.9 %copy.42 = bf16[128,1024]{1,0:T(8,128)(2,1)} copy(bf16[128,1024]{0,1:T(8,128)(2,1)S(1)} %bitcast.36) | data formatting | bytes 524288 | tf_op jit(solution)/shard_map/reshape | solution.py:202
  (12 shorter events, 0.1 us)
Async XLA Ops:
  2.2 2.4 %copy-start.4 = (f32[128,8]{0,1:T(8,128)S(1)}, f32[128,8]{0,1:T(8,128)}, u32[]{:S(2)}) copy-start(f32[128,8]{0,1:T(8,128)} %param.9) | copy-start | bytes 12292
  2.2 5.3 %collective-permute-start = (bf16[9,1024]{1,0:T(8,128)(2,1)S(1)}, bf16[9,1024]{1,0:T(8,128)(2,1)S(1)}, u32[]{:S(2)}, u32[]{:S(2)}) collective-permute-start(bf16[9,1024]{1,0:T(8,128)(2,1)S(1)} %pad_maximum_fusion), channel_id=1, source_target_pairs={{0,1},{1,2},{2,3},{3,4},{4,5},{5,6},{6,7},{7,8},{8,9},{9,10},{10,1... | collective-permute-start | bytes 55304 | tf_op jit(solution)/shard_map/ppermute | solution.py:150
  4.6 1.2 %copy-start.1 = (bf16[128,1024]{1,0:T(8,128)(2,1)S(1)}, bf16[128,1024]{1,0:T(8,128)(2,1)}, u32[]{:S(2)}) copy-start(bf16[128,1024]{1,0:T(8,128)(2,1)} %param.7) | copy-start | bytes 786436
  5.8 1.0 %copy-start.2 = (bf16[128,1024]{1,0:T(8,128)(2,1)S(1)}, bf16[128,1024]{1,0:T(8,128)(2,1)}, u32[]{:S(2)}) copy-start(bf16[128,1024]{1,0:T(8,128)(2,1)} %param.8) | copy-start | bytes 786436
  11.9 18.1 %all-to-all-start = ((bf16[8,400,128]{2,1,0:T(8,128)(2,1)}), bf16[8,400,128]{2,1,0:T(8,128)(2,1)S(1)}, u32[]{:S(2)}, u32[]{:S(2)}) async-start(bf16[8,400,128]{2,1,0:T(8,128)(2,1)} %concatenate.8), calls=%async_computation | async-start | bytes 1638400 | tf_op jit(solution)/shard_map/all_to_all | solution.py:159
  17.9 0.7 %copy-start.3 = (bf16[3,4,1024]{2,1,0:T(4,128)(2,1)S(1)}, bf16[3,4,1024]{2,1,0:T(4,128)(2,1)}, u32[]{:S(2)}) copy-start(bf16[3,4,1024]{2,1,0:T(4,128)(2,1)} %param.10) | copy-start | bytes 73732
  30.0 0.9 %copy-start = (bf16[8,400,128]{2,1,0:T(8,128)(2,1)}, bf16[8,400,128]{2,1,0:T(8,128)(2,1)S(1)}, u32[]{:S(2)}) copy-start(bf16[8,400,128]{2,1,0:T(8,128)(2,1)S(1)} %all-to-all-done.raw_ref) | copy-start | bytes 2457604
  41.1 5.2 %collective-permute-start.1 = (f32[128,128]{1,0:T(8,128)S(1)}, f32[128,128]{1,0:T(8,128)S(1)}, u32[]{:S(2)}, u32[]{:S(2)}) collective-permute-start(f32[128,128]{1,0:T(8,128)S(1)} %slice_bitcast_fusion), channel_id=1, source_target_pairs={{0,8},{1,9},{2,10},{3,11},{4,12},{5,13},{6,14},{7,15},{8,0},{9,1},... | collective-permute-start | bytes 196616 | tf_op jit(solution)/shard_map/ppermute | solution.py:180
